TPU v7x, 32 devices: a whole 2x2x4 slice. The times are simulated.
32 devices in a mesh: dp: 8 (over z, x), row: 2 (over core), col: 2 (over y).
Axes of the slice: x: 2, y: 2, z: 4, core: 2. Of those that a mesh axis runs over, the one named last changes fastest.
Arguments:
- tokens: bfloat16 [2, 8, 256, 2048], P(None, None, 'dp', ('row', 'col')), may hold values from -57 to 57
- lengths: int32 [2, 8], replicated, may hold values from 64 to 256, as said below
- deal_order: int32 [2, 8], replicated, may hold values from 0 to 7, each once within a row
- attention_gain: float32 [2048], P(('row', 'col')), may hold values from 0.25 to 1.75
- query_weight: bfloat16 [2048, 2048], P('row', 'col'), may hold values from -0.1875 to 0.1875
- key_weight: bfloat16 [2048, 2048], P('row', 'col'), may hold values from -0.1875 to 0.1875
- value_weight: bfloat16 [2048, 2048], P('row', 'col'), may hold values from -0.125 to 0.125
- output_weight: bfloat16 [2048, 2048], P('col', 'row'), may hold values from -0.25 to 0.25
- feed_gain: float32 [2048], P(('row', 'col')), may hold values from 0.25 to 1.75
- gate_weight: bfloat16 [2048, 8192], P('row', 'col'), may hold values from -0.125 to 0.125
- up_weight: bfloat16 [2048, 8192], P('row', 'col'), may hold values from -0.125 to 0.125
- down_weight: bfloat16 [8192, 2048], P('col', 'row'), may hold values from -0.09375 to 0.09375
- cotangent: bfloat16 [2, 8, 256, 2048], P(None, 'dp', None, ('row', 'col')), may hold values from -6 to 6
Outputs:
- layer_output: bfloat16 [2, 8, 256, 2048], P(None, None, 'dp', ('row', 'col'))
- tokens_grad: bfloat16 [2, 8, 256, 2048], P(None, None, 'dp', ('row', 'col'))
- attention_gain_grad: float32 [2048], P(('row', 'col', 'dp'))
- query_grad: float32 [2048, 2048], P(('row', 'dp'), 'col')
- key_grad: float32 [2048, 2048], P(('row', 'dp'), 'col')
- value_grad: float32 [2048, 2048], P(('row', 'dp'), 'col')
- output_grad: float32 [2048, 2048], P(('col', 'dp'), 'row')
- feed_gain_grad: float32 [2048], P(('row', 'col', 'dp'))
- gate_grad: float32 [2048, 8192], P(('row', 'dp'), 'col')
- up_grad: float32 [2048, 8192], P(('row', 'dp'), 'col')
- down_grad: float32 [8192, 2048], P(('col', 'dp'), 'row')
Inputs may be any that keep to these rules, and one draw needn't show every extreme that they name: `lengths`: in each micro-batch one sequence has exactly 256 tokens. `deal_order`: each row holds every number of 0 to 7 once.
All inputs are finite; a program needn't handle non-finite values.
Results may differ from a plain program's by a relative error of at most 0.023.
Values may be sent and summed in bfloat16 or wider, within the bound.
A program may use at most 256 MiB of HBM per device.

v0:
```python
import math
import jax
import jax.numpy as jnp
from jax import lax
from jax.sharding import PartitionSpec as P

D = 2048
HEADS = 32
HEAD_DIM = 64
SL = 256
MICRO = 2
EPSILON = 1e-05
ROPE_THETA = 130000.0
MASKED_SCORE = -1000000000.0


def rope_tables(slot_count, head_width):
    half_width = head_width // 2
    frequency = jnp.exp(
        jnp.arange(half_width, dtype=jnp.float32) * (-2.0 * math.log(ROPE_THETA) / head_width)
    )
    angles = jnp.arange(slot_count, dtype=jnp.float32)[:, None] * frequency[None, :]
    return (jnp.cos(angles)[:, None, :], jnp.sin(angles)[:, None, :])


def rotate(values, cosine_table, sine_table):
    half_width = values.shape[-1] // 2
    first_half = values[..., :half_width]
    second_half = values[..., half_width:]
    return jnp.concatenate(
        [
            first_half * cosine_table - second_half * sine_table,
            second_half * cosine_table + first_half * sine_table,
        ],
        axis=-1,
    )


def unrotate(grads, cosine_table, sine_table):
    half_width = grads.shape[-1] // 2
    first_half = grads[..., :half_width]
    second_half = grads[..., half_width:]
    return jnp.concatenate(
        [
            first_half * cosine_table + second_half * sine_table,
            second_half * cosine_table - first_half * sine_table,
        ],
        axis=-1,
    )


def masked_scores(queries, key_rows, length):
    positions = jnp.arange(SL, dtype=jnp.int32)
    allowed = (positions[None, :] <= positions[:, None]) & (positions[None, :] < length)
    scores = jnp.einsum(
        "qhd,khd->hqk", queries, key_rows, preferred_element_type=jnp.float32
    ) * HEAD_DIM ** (-0.5)
    return jnp.where(allowed[None], scores, MASKED_SCORE)


def attend_forward(queries, key_rows, values, length):
    scores = masked_scores(queries, key_rows, length)
    row_top = jnp.max(scores, axis=-1, keepdims=True)
    exp_scores = jnp.exp(scores - row_top)
    row_total = jnp.sum(exp_scores, axis=-1, keepdims=True)
    softmax_out = (exp_scores / row_total).astype(jnp.bfloat16)
    mixed_heads = jnp.einsum(
        "hqk,khd->qhd", softmax_out, values, preferred_element_type=jnp.float32
    )
    return (mixed_heads, row_top + jnp.log(row_total))


def attend_backward(queries, key_rows, values, length, log_total, mixed_grad):
    softmax_out = jnp.exp(masked_scores(queries, key_rows, length) - log_total)
    softmax_grad = jnp.einsum(
        "qhd,khd->hqk", mixed_grad, values, preferred_element_type=jnp.float32
    )
    values_grad = jnp.einsum(
        "hqk,qhd->khd",
        softmax_out.astype(jnp.bfloat16),
        mixed_grad,
        preferred_element_type=jnp.float32,
    )
    row_inner = jnp.sum(softmax_out * softmax_grad, axis=-1, keepdims=True)
    scores_grad = (softmax_out * (softmax_grad - row_inner)).astype(jnp.bfloat16)
    queries_grad = jnp.einsum(
        "hqk,khd->qhd", scores_grad, key_rows, preferred_element_type=jnp.float32
    ) * HEAD_DIM ** (-0.5)
    keys_grad = jnp.einsum(
        "hqk,qhd->khd", scores_grad, queries, preferred_element_type=jnp.float32
    ) * HEAD_DIM ** (-0.5)
    return (queries_grad, keys_grad, values_grad)


def column_gather(values):
    return lax.all_gather(values, "col", axis=1, tiled=True)


def row_scatter(stacked):
    return lax.psum_scatter(stacked, "row", scatter_dimension=2, tiled=True)


def row_gather(stacked):
    return lax.all_gather(stacked, "row", axis=2, tiled=True)


def column_scatter(partial_rows):
    return lax.psum_scatter(
        partial_rows.astype(jnp.bfloat16), "col", scatter_dimension=1, tiled=True
    ).astype(jnp.float32)


def feature_total(row_values):
    return lax.psum(row_values, ("row", "col"))


def norm_scale(values):
    return lax.rsqrt(feature_total(jnp.sum(values * values, axis=1)) / D + EPSILON)


def norm_backward(normed_grad, values, inverse_rms, gain_vector, upstream):
    gain_piece = jnp.sum(normed_grad * values * inverse_rms[:, None], axis=0)
    feature_dot = feature_total(jnp.sum(normed_grad * gain_vector * values, axis=1))
    result = (
        upstream
        + normed_grad * gain_vector * inverse_rms[:, None]
        - values * (inverse_rms**3 * feature_dot / D)[:, None]
    )
    return (result, gain_piece)


def per_device(
    tokens,
    lengths,
    deal_order,
    attention_gain,
    query_weight,
    key_weight,
    value_weight,
    output_weight,
    feed_gain,
    gate_weight,
    up_weight,
    down_weight,
    cotangent,
):
    head_shape = (SL, HEADS // (lax.axis_size("row") * lax.axis_size("col")), HEAD_DIM)
    dealt_rows = lax.all_to_all(
        jnp.take_along_axis(tokens, deal_order[:, :, None, None], axis=1),
        "dp",
        split_axis=1,
        concat_axis=2,
        tiled=True,
    )
    own_order = lax.dynamic_slice_in_dim(deal_order, lax.axis_index("dp"), 1, 1)
    own_lengths = jnp.take_along_axis(lengths, own_order, axis=1)[:, 0]
    cosine_table, sine_table = rope_tables(SL, HEAD_DIM)
    qkv_weights = jnp.stack((query_weight, key_weight, value_weight))
    pair_weights = jnp.stack((gate_weight, up_weight))
    qkv_grad_sum = jnp.zeros(qkv_weights.shape, jnp.float32)
    output_grad_sum = jnp.zeros(output_weight.shape, jnp.float32)
    pair_grad_sum = jnp.zeros(pair_weights.shape, jnp.float32)
    down_grad_sum = jnp.zeros(down_weight.shape, jnp.float32)
    attention_gain_sum = jnp.zeros(attention_gain.shape, jnp.float32)
    feed_gain_sum = jnp.zeros(feed_gain.shape, jnp.float32)
    row_positions = jnp.arange(SL, dtype=jnp.int32)
    output_blocks = []
    grad_blocks = []
    for micro_index in range(MICRO):
        length = own_lengths[micro_index]
        residual_in = dealt_rows[micro_index, 0].astype(jnp.float32)
        upstream = (
            cotangent[micro_index, 0].astype(jnp.float32)
            * (row_positions < length).astype(jnp.float32)[:, None]
        )
        inverse_first = norm_scale(residual_in)
        normed_first = (residual_in * inverse_first[:, None] * attention_gain).astype(jnp.bfloat16)
        normed_first_all = column_gather(normed_first)
        projected = row_scatter(
            jnp.einsum(
                "rd,kde->kre", normed_first_all, qkv_weights, preferred_element_type=jnp.float32
            )
        )
        queries = rotate(projected[0].reshape(head_shape), cosine_table, sine_table).astype(
            jnp.bfloat16
        )
        key_rows = rotate(projected[1].reshape(head_shape), cosine_table, sine_table).astype(
            jnp.bfloat16
        )
        values = projected[2].reshape(head_shape).astype(jnp.bfloat16)
        mixed_heads, log_total = attend_forward(queries, key_rows, values, length)
        mixed_all = row_gather(mixed_heads.reshape(1, SL, -1).astype(jnp.bfloat16))[0]
        middle = residual_in + column_scatter(
            jnp.dot(mixed_all, output_weight, preferred_element_type=jnp.float32)
        )
        inverse_second = norm_scale(middle)
        normed_second = (middle * inverse_second[:, None] * feed_gain).astype(jnp.bfloat16)
        normed_second_all = column_gather(normed_second)
        gate_up = row_scatter(
            jnp.einsum(
                "rd,kde->kre", normed_second_all, pair_weights, preferred_element_type=jnp.float32
            )
        )
        swish_gate = gate_up[0] / (1.0 + jnp.exp(-gate_up[0]))
        hidden = (swish_gate * gate_up[1]).astype(jnp.bfloat16)
        hidden_all = row_gather(hidden[None])[0]
        layer_rows = middle + column_scatter(
            jnp.dot(hidden_all, down_weight, preferred_element_type=jnp.float32)
        )
        output_blocks.append(layer_rows.astype(jnp.bfloat16))
        top_all = column_gather(upstream.astype(jnp.bfloat16))
        down_grad_sum = down_grad_sum + jnp.einsum(
            "rf,rd->fd", hidden_all, top_all, preferred_element_type=jnp.float32
        )
        hidden_grad = row_scatter(
            jnp.einsum("rd,fd->rf", top_all, down_weight, preferred_element_type=jnp.float32)[None]
        )[0]
        sigmoid_gate = 1.0 / (1.0 + jnp.exp(-gate_up[0]))
        gate_grad = (
            hidden_grad * gate_up[1] * sigmoid_gate * (1.0 + gate_up[0] * (1.0 - sigmoid_gate))
        )
        pair_grad_all = row_gather(
            jnp.stack((gate_grad, hidden_grad * swish_gate)).astype(jnp.bfloat16)
        )
        pair_grad_sum = pair_grad_sum + jnp.einsum(
            "rd,kre->kde", normed_second_all, pair_grad_all, preferred_element_type=jnp.float32
        )
        second_grad = column_scatter(
            jnp.einsum(
                "kre,kde->rd", pair_grad_all, pair_weights, preferred_element_type=jnp.float32
            )
        )
        middle_grad, gain_piece = norm_backward(
            second_grad, middle, inverse_second, feed_gain, upstream
        )
        feed_gain_sum = feed_gain_sum + gain_piece
        branch_all = column_gather(middle_grad.astype(jnp.bfloat16))
        output_grad_sum = output_grad_sum + jnp.einsum(
            "rh,rd->hd", mixed_all, branch_all, preferred_element_type=jnp.float32
        )
        mixed_grad = row_scatter(
            jnp.einsum("rd,hd->rh", branch_all, output_weight, preferred_element_type=jnp.float32)[
                None
            ]
        )[0]
        queries_grad, keys_grad, values_grad = attend_backward(
            queries,
            key_rows,
            values,
            length,
            log_total,
            mixed_grad.reshape(head_shape).astype(jnp.bfloat16),
        )
        turned_back = jnp.stack(
            (
                unrotate(queries_grad, cosine_table, sine_table),
                unrotate(keys_grad, cosine_table, sine_table),
                values_grad,
            )
        )
        three_all = row_gather(turned_back.reshape(3, SL, -1).astype(jnp.bfloat16))
        qkv_grad_sum = qkv_grad_sum + jnp.einsum(
            "rd,kre->kde", normed_first_all, three_all, preferred_element_type=jnp.float32
        )
        first_grad = column_scatter(
            jnp.einsum("kre,kde->rd", three_all, qkv_weights, preferred_element_type=jnp.float32)
        )
        input_grad, gain_piece = norm_backward(
            first_grad, residual_in, inverse_first, attention_gain, middle_grad
        )
        attention_gain_sum = attention_gain_sum + gain_piece
        grad_blocks.append(input_grad.astype(jnp.bfloat16))
    reduced = (
        lax.psum_scatter(
            attention_gain_sum.astype(jnp.bfloat16), "dp", scatter_dimension=0, tiled=True
        ).astype(jnp.float32),
        lax.psum_scatter(
            qkv_grad_sum[0].astype(jnp.bfloat16), "dp", scatter_dimension=0, tiled=True
        ).astype(jnp.float32),
        lax.psum_scatter(
            qkv_grad_sum[1].astype(jnp.bfloat16), "dp", scatter_dimension=0, tiled=True
        ).astype(jnp.float32),
        lax.psum_scatter(
            qkv_grad_sum[2].astype(jnp.bfloat16), "dp", scatter_dimension=0, tiled=True
        ).astype(jnp.float32),
        lax.psum_scatter(
            output_grad_sum.astype(jnp.bfloat16), "dp", scatter_dimension=0, tiled=True
        ).astype(jnp.float32),
        lax.psum_scatter(
            feed_gain_sum.astype(jnp.bfloat16), "dp", scatter_dimension=0, tiled=True
        ).astype(jnp.float32),
        lax.psum_scatter(
            pair_grad_sum[0].astype(jnp.bfloat16), "dp", scatter_dimension=0, tiled=True
        ).astype(jnp.float32),
        lax.psum_scatter(
            pair_grad_sum[1].astype(jnp.bfloat16), "dp", scatter_dimension=0, tiled=True
        ).astype(jnp.float32),
        lax.psum_scatter(
            down_grad_sum.astype(jnp.bfloat16), "dp", scatter_dimension=0, tiled=True
        ).astype(jnp.float32),
    )
    returned_out, returned_grad = (
        lax.all_to_all(
            jnp.stack(output_blocks)[:, None], "dp", split_axis=2, concat_axis=1, tiled=True
        ),
        lax.all_to_all(
            jnp.stack(grad_blocks)[:, None], "dp", split_axis=2, concat_axis=1, tiled=True
        ),
    )
    slot_of = jnp.argsort(deal_order, axis=1)[:, :, None, None]
    layer_output = jnp.take_along_axis(returned_out, slot_of, axis=1)
    tokens_grad = jnp.take_along_axis(returned_grad, slot_of, axis=1)
    return (
        layer_output,
        tokens_grad,
        reduced[0],
        reduced[1],
        reduced[2],
        reduced[3],
        reduced[4],
        reduced[5],
        reduced[6],
        reduced[7],
        reduced[8],
    )


def solution(mesh):
    in_specs = (
        P(None, None, "dp", ("row", "col")),
        P(),
        P(),
        P(("row", "col")),
        P("row", "col"),
        P("row", "col"),
        P("row", "col"),
        P("col", "row"),
        P(("row", "col")),
        P("row", "col"),
        P("row", "col"),
        P("col", "row"),
        P(None, "dp", None, ("row", "col")),
    )
    out_specs = (
        P(None, None, "dp", ("row", "col")),
        P(None, None, "dp", ("row", "col")),
        P(("row", "col", "dp")),
        P(("row", "dp"), "col"),
        P(("row", "dp"), "col"),
        P(("row", "dp"), "col"),
        P(("col", "dp"), "row"),
        P(("row", "col", "dp")),
        P(("row", "dp"), "col"),
        P(("row", "dp"), "col"),
        P(("col", "dp"), "row"),
    )
    return jax.shard_map(
        per_device, mesh=mesh, in_specs=in_specs, out_specs=out_specs, check_vma=False
    )
```

profile of v0, /device:TPU:0, one launch (start us, length us, event | category | flops | bytes accessed | tf_op | source)
XLA Modules:
  0.0 1240.4 jit_solution(1370745527233818062)
XLA Ops:
  11.4 7.3 all-to-all-start
  33.5 7.5 all-reduce.5
  41.7 9.3 all_gather.52
  51.8 6.3 convolution_bitcast_fusion.4
  58.2 8.5 all_gather.48
  67.5 6.4 convolution_bitcast_fusion.5
  102.4 10.7 all_gather.60
  113.9 7.9 convolution_bitcast_fusion.2
  121.8 12.0 copy.158
  133.8 12.3 copy.159
  147.9 7.0 all-reduce.4
  158.1 8.9 all_gather.54
  167.8 10.3 convolution_bitcast_fusion
  178.1 7.8 all_gather.56
  186.7 9.7 convolution_bitcast_fusion.3
  197.4 7.0 all_gather.50
  205.2 11.7 convolution_bitcast_fusion.1
  224.1 10.2 reduce-scatter.38.cloned.1.call-done
  241.6 9.2 all-gather.15.cloned.1.call-done
  250.8 10.1 fusion.24
  261.0 6.1 all-gather.11.cloned.1.call-done
  267.1 10.1 fusion.23
  280.4 7.2 fusion.20
  287.7 11.2 reduce-scatter.60.cloned.1.call-done
  298.9 17.5 %reduce-scatter.52.cloned.1.call-done = bf16[256,512]{1,0:T(8,128)(2,1)} async-done(((bf16[256,1024]{1,0:T(8,128)(2,1)}), bf16[256,512]{1,0:T(8,128)(2,1)}) %reduce-scatter.52.cloned.1.call-update) | async-done | bytes 262160 | tf_op jit(solution)/shard_map/reduce_scatter | solution.py:108
  318.6 7.0 all-reduce.3
  328.0 5.5 reduce-scatter.48.cloned.1.call-done
  336.2 8.7 all_gather.58
  347.5 8.1 all_gather.62
  419.1 8.0 all-gather.7.cloned.1.call-done
  427.2 7.2 fusion.17
  458.9 9.3 fusion.5
  468.3 11.7 add_convert_fusion.1
  481.0 15.7 %fusion.74 = f32[2,4096,1024]{2,1,0:T(8,128)} fusion(bf16[2,256,4096]{1,2,0:T(8,128)(2,1)} %all-gather.11.cloned.1.call-done, bf16[256,1024]{1,0:T(8,128)(2,1)S(1)} %copy-done.32), kind=kOutput, calls=%fused_computation.147 | convolution fusion | flops 4294967296 | bytes 38273024 | tf_op jit(solution)/shard_map/rd,kre->kde/dot_general | solution.py:225
  496.8 19.1 %fusion = bf16[2,1024,4096]{1,2,0:T(8,128)(2,1)} fusion(f32[2,4096,1024]{2,1,0:T(8,128)} %fusion.74, bf16[2,256,4096]{1,2,0:T(8,128)(2,1)S(1)} %copy-done.23, bf16[256,1024]{1,0:T(8,128)(2,1)S(1)} %copy-done.30), kind=kOutput, calls=%fused_computation.5 | convolution fusion | flops 4311744512 | bytes 55050240 | tf_op jit(solution)/shard_map/rd,kre->kde/dot_general | solution.py:225
  515.9 11.7 slice_bitcast_fusion
  527.7 11.3 copy.220
  539.0 11.6 copy.218
  552.9 7.7 all-reduce.2
  563.7 5.9 all-to-all-start.1
  572.2 21.8 %all-to-all-done.1 = bf16[2,1,256,512]{3,0,1,2:T(2,128)(2,1)S(1)} async-done(((bf16[2,1,256,512]{3,0,1,2:T(2,128)(2,1)}), bf16[2,1,256,512]{3,0,1,2:T(2,128)(2,1)S(1)}, u32[]{:S(2)}, u32[]{:S(2)}) %all-to-all-start.1) | async-done | bytes 524320 | tf_op jit(solution)/shard_map/all_to_all | solution.py:303
  601.1 22.1 %all-reduce.6 = (bf16[512]{0:T(512)(128)(2,1)S(1)}, bf16[512]{0:T(512)(128)(2,1)S(1)}) all-reduce(bf16[512]{0:T(512)(128)(2,1)S(1)} %add_convert_fusion.15, bf16[512]{0:T(512)(128)(2,1)S(1)} %add_convert_fusion.14), channel_id=18, replica_groups=mesh['dp'=8,'row'=2,'col'=2] {'dp'}, use_global_device_ids=true, to_apply=%region_41.43.clone | all-reduce | flops 1024 | bytes 4096
  626.9 6.0 reduce-scatter.74.cloned.1.call-done
  635.0 68.9 %reduce-scatter.72.cloned.1.call-done = bf16[128,1024]{1,0:T(8,128)(2,1)} async-done(((bf16[1024,1024]{1,0:T(8,128)(2,1)}), bf16[128,1024]{1,0:T(8,128)(2,1)}) %reduce-scatter.72.cloned.1.call-update) | async-done | bytes 262160
  705.9 68.8 %reduce-scatter.70.cloned.1.call-done = bf16[128,1024]{1,0:T(8,128)(2,1)} async-done(((bf16[1024,1024]{1,0:T(8,128)(2,1)}), bf16[128,1024]{1,0:T(8,128)(2,1)}) %reduce-scatter.70.cloned.1.call-update) | async-done | bytes 262160
  776.7 149.5 %reduce-scatter.68.cloned.1.call-done = bf16[512,1024]{1,0:T(8,128)(2,1)} async-done(((bf16[4096,1024]{1,0:T(8,128)(2,1)}), bf16[512,1024]{1,0:T(8,128)(2,1)}) %reduce-scatter.68.cloned.1.call-update) | async-done | bytes 1048592 | tf_op jit(solution)/shard_map/reduce_scatter | solution.py:298
  929.0 149.4 %reduce-scatter.78.cloned.1.call-done = bf16[128,4096]{1,0:T(8,128)(2,1)} async-done(((bf16[1024,4096]{1,0:T(8,128)(2,1)}), bf16[128,4096]{1,0:T(8,128)(2,1)}) %reduce-scatter.78.cloned.1.call-update) | async-done | bytes 1048592
  1081.6 148.4 %reduce-scatter.76.cloned.1.call-done = bf16[128,4096]{1,0:T(8,128)(2,1)} async-done(((bf16[1024,4096]{1,0:T(8,128)(2,1)}), bf16[128,4096]{1,0:T(8,128)(2,1)}) %reduce-scatter.76.cloned.1.call-update) | async-done | bytes 1048592
  (386 shorter events, 208.6 us)
Async XLA Ops:
  7.2 84.0 %copy-start = (bf16[1024,1024]{1,0:T(8,128)(2,1)S(1)}, bf16[1024,1024]{1,0:T(8,128)(2,1)}, u32[]{:S(2)}) copy-start(bf16[1024,1024]{1,0:T(8,128)(2,1)} %param.22) | copy-start | bytes 6291460
  11.4 21.7 %all-to-all-start = ((bf16[2,8,32,512]{3,2,0,1:T(8,128)(2,1)}), bf16[2,8,32,512]{3,2,0,1:T(8,128)(2,1)S(1)}, u32[]{:S(2)}, u32[]{:S(2)}) async-start(bf16[2,8,32,512]{3,2,0,1:T(8,128)(2,1)} %copy.151), calls=%async_computation | async-start | bytes 1048576 | tf_op jit(solution)/shard_map/all_to_all | solution.py:148
  18.6 62.7 %reduce-scatter.42.cloned.1.call-start = ((), (), s32[]{:S(2)}) async-start(), calls=%async_computation.31 | async-start | bytes 4718592 | tf_op jit(solution)/shard_map/reduce_scatter | solution.py:100
  26.6 15.0 %copy-start.63 = (f32[512]{0:T(512)S(1)}, f32[512]{0:T(512)}, u32[]{:S(2)}) copy-start(f32[512]{0:T(512)} %param.18) | copy-start | bytes 6148
  41.0 10.1 copy-start.73
  58.2 25.3 %reduce-scatter.34.cloned.1.call-start = ((), (), s32[]{:S(2)}) async-start(), calls=%async_computation.26 | async-start | bytes 4718592 | tf_op jit(solution)/shard_map/reduce_scatter | solution.py:100
  73.9 72.2 %reduce-scatter.36.cloned.1.call-start = ((), (), s32[]{:S(2)}) async-start(), calls=%async_computation.27 | async-start | bytes 786432 | tf_op jit(solution)/shard_map/reduce_scatter | solution.py:108
  79.0 22.1 %copy-start.69 = (f32[256]{0:T(256)}, f32[256]{0:T(256)S(1)}, u32[]{:S(2)}) copy-start(f32[256]{0:T(256)S(1)} %get-tuple-element.152) | copy-start | bytes 3076
  79.0 22.1 %copy-start.71 = (f32[256]{0:T(256)}, f32[256]{0:T(256)S(1)}, u32[]{:S(2)}) copy-start(f32[256]{0:T(256)S(1)} %get-tuple-element.153) | copy-start | bytes 3076
  92.7 53.4 %reduce-scatter.44.cloned.1.call-start = ((), (), s32[]{:S(2)}) async-start(), calls=%async_computation.32 | async-start | bytes 786432 | tf_op jit(solution)/shard_map/reduce_scatter | solution.py:108
  101.1 116.4 %reduce-scatter.58.cloned.1.call-start = ((), (), s32[]{:S(2)}) async-start(), calls=%async_computation.42 | async-start | bytes 6291456 | tf_op jit(solution)/shard_map/reduce_scatter | solution.py:100
  121.8 95.7 %reduce-scatter.46.cloned.1.call-start = ((), (), s32[]{:S(2)}) async-start(), calls=%async_computation.33 | async-start | bytes 12582912 | tf_op jit(solution)/shard_map/reduce_scatter | solution.py:100
  133.8 22.4 %copy-start.59 = (f32[512]{0:T(512)S(1)}, f32[512]{0:T(512)}, u32[]{:S(2)}) copy-start(f32[512]{0:T(512)} %param.23) | copy-start | bytes 6148
  156.2 10.8 copy-start.65
  178.1 46.0 %reduce-scatter.50.cloned.1.call-start = ((), (), s32[]{:S(2)}) async-start(), calls=%async_computation.36 | async-start | bytes 6291456 | tf_op jit(solution)/shard_map/reduce_scatter | solution.py:100
  196.5 37.8 %reduce-scatter.38.cloned.1.call-start = ((), (), s32[]{:S(2)}) async-start(), calls=%async_computation.28 | async-start | bytes 12582912 | tf_op jit(solution)/shard_map/reduce_scatter | solution.py:100
  217.0 33.8 %all-gather.15.cloned.1.call-start = ((), (), s32[]{:S(2)}) async-start(), calls=%async_computation.43 | async-start | bytes 6291456 | tf_op jit(solution)/shard_map/all_gather | solution.py:104
  224.0 43.1 %all-gather.11.cloned.1.call-start = ((), (), s32[]{:S(2)}) async-start(), calls=%async_computation.37 | async-start | bytes 6291456 | tf_op jit(solution)/shard_map/all_gather | solution.py:104
  240.8 39.6 %all-gather.9.cloned.1.call-start = ((), (), s32[]{:S(2)}) async-start(), calls=%async_computation.34 | async-start | bytes 3145728 | tf_op jit(solution)/shard_map/all_gather | solution.py:104
  241.5 57.3 %reduce-scatter.60.cloned.1.call-start = ((), (), s32[]{:S(2)}) async-start(), calls=%async_computation.44 | async-start | bytes 786432 | tf_op jit(solution)/shard_map/reduce_scatter | solution.py:108
  261.0 55.4 %reduce-scatter.52.cloned.1.call-start = ((), (), s32[]{:S(2)}) async-start(), calls=%async_computation.38 | async-start | bytes 786432 | tf_op jit(solution)/shard_map/reduce_scatter | solution.py:108
  277.2 39.1 %copy-start.10 = (bf16[256,512]{1,0:T(8,128)(2,1)S(1)}, bf16[256,512]{1,0:T(8,128)(2,1)}, u32[]{:S(2)}) copy-start(bf16[256,512]{1,0:T(8,128)(2,1)} %reduce-scatter.44.cloned.1.call-done) | copy-start | bytes 786436
  277.2 56.3 %reduce-scatter.48.cloned.1.call-start = ((), (), s32[]{:S(2)}) async-start(), calls=%async_computation.35 | async-start | bytes 786432 | tf_op jit(solution)/shard_map/reduce_scatter | solution.py:108
  287.6 72.9 %reduce-scatter.54.cloned.1.call-start = ((), (), s32[]{:S(2)}) async-start(), calls=%async_computation.39 | async-start | bytes 1572864 | tf_op jit(solution)/shard_map/reduce_scatter | solution.py:100
  347.4 22.8 %reduce-scatter.62.cloned.1.call-start = ((), (), s32[]{:S(2)}) async-start(), calls=%async_computation.45 | async-start | bytes 1572864 | tf_op jit(solution)/shard_map/reduce_scatter | solution.py:100
  358.1 45.5 %all-gather.13.cloned.1.call-start = ((), (), s32[]{:S(2)}) async-start(), calls=%async_computation.40 | async-start | bytes 2359296 | tf_op jit(solution)/shard_map/all_gather | solution.py:104
  391.3 22.5 %all-gather.17.cloned.1.call-start = ((), (), s32[]{:S(2)}) async-start(), calls=%async_computation.46 | async-start | bytes 2359296 | tf_op jit(solution)/shard_map/all_gather | solution.py:104
  402.8 24.4 %all-gather.7.cloned.1.call-start = ((), (), s32[]{:S(2)}) async-start(), calls=%async_computation.29 | async-start | bytes 3145728 | tf_op jit(solution)/shard_map/all_gather | solution.py:104
  403.6 147.2 %reduce-scatter.56.cloned.1.call-start = ((), (), s32[]{:S(2)}) async-start(), calls=%async_computation.41 | async-start | bytes 786432 | tf_op jit(solution)/shard_map/reduce_scatter | solution.py:108
  408.9 141.8 %reduce-scatter.64.cloned.1.call-start = ((), (), s32[]{:S(2)}) async-start(), calls=%async_computation.47 | async-start | bytes 786432 | tf_op jit(solution)/shard_map/reduce_scatter | solution.py:108
  419.1 15.6 %copy-start.21 = (bf16[256,1024]{1,0:T(8,128)(2,1)S(1)}, bf16[256,1024]{1,0:T(8,128)(2,1)}, u32[]{:S(2)}) copy-start(bf16[256,1024]{1,0:T(8,128)(2,1)} %copy-done.20) | copy-start | bytes 1572868
  419.1 141.5 %reduce-scatter.40.cloned.1.call-start = ((), (), s32[]{:S(2)}) async-start(), calls=%async_computation.30 | async-start | bytes 786432 | tf_op jit(solution)/shard_map/reduce_scatter | solution.py:108
  434.4 164.9 %reduce-scatter.66.cloned.1.call-start = ((), (), s32[]{:S(2)}) async-start(), calls=%async_computation.48 | async-start | bytes 2359296 | tf_op jit(solution)/shard_map/reduce_scatter | solution.py:286
  437.7 195.2 %reduce-scatter.74.cloned.1.call-start = ((), (), s32[]{:S(2)}) async-start(), calls=%async_computation.52 | async-start | bytes 2359296
  450.7 253.1 %reduce-scatter.72.cloned.1.call-start = ((), (), s32[]{:S(2)}) async-start(), calls=%async_computation.51 | async-start | bytes 2359296
  454.7 319.9 %reduce-scatter.70.cloned.1.call-start = ((), (), s32[]{:S(2)}) async-start(), calls=%async_computation.50 | async-start | bytes 2359296
  457.4 10.9 copy-start.18
  457.4 468.8 %reduce-scatter.68.cloned.1.call-start = ((), (), s32[]{:S(2)}) async-start(), calls=%async_computation.49 | async-start | bytes 9437184 | tf_op jit(solution)/shard_map/reduce_scatter | solution.py:298
  480.0 16.8 %copy-start.30 = (bf16[256,1024]{1,0:T(8,128)(2,1)S(1)}, bf16[256,1024]{1,0:T(8,128)(2,1)}, u32[]{:S(2)}) copy-start(bf16[256,1024]{1,0:T(8,128)(2,1)} %copy-done.29) | copy-start | bytes 1572868
  480.0 598.4 %reduce-scatter.78.cloned.1.call-start = ((), (), s32[]{:S(2)}) async-start(), calls=%async_computation.54 | async-start | bytes 9437184
  481.0 15.7 %copy-start.23 = (bf16[2,256,4096]{1,2,0:T(8,128)(2,1)S(1)}, bf16[2,256,4096]{1,2,0:T(8,128)(2,1)}, u32[]{:S(2)}) copy-start(bf16[2,256,4096]{1,2,0:T(8,128)(2,1)} %all-gather.15.cloned.1.call-done) | copy-start | bytes 12582916
  539.0 691.1 %reduce-scatter.76.cloned.1.call-start = ((), (), s32[]{:S(2)}) async-start(), calls=%async_computation.53 | async-start | bytes 9437184
  550.7 11.6 copy-start.39
  563.7 30.3 %all-to-all-start.1 = ((bf16[2,1,256,512]{3,0,1,2:T(2,128)(2,1)}), bf16[2,1,256,512]{3,0,1,2:T(2,128)(2,1)S(1)}, u32[]{:S(2)}, u32[]{:S(2)}) async-start(bf16[2,1,256,512]{3,0,1,2:T(2,128)(2,1)} %copy.161), calls=%async_computation.9 | async-start | bytes 1048576 | tf_op jit(solution)/shard_map/all_to_all | solution.py:303
  570.4 27.6 %copy-start.85 = (u32[32]{0:T(128)S(1)}, u32[32]{0:T(128)}, u32[]{:S(2)}) copy-start(u32[32]{0:T(128)} %constant.126) | copy-start | bytes 388
  570.5 28.8 %copy-start.79 = (f32[512]{0:T(512)S(1)}, f32[512]{0:T(512)}, u32[]{:S(2)}) copy-start(f32[512]{0:T(512)} %get-tuple-element.60) | copy-start | bytes 6148
  570.5 28.8 %copy-start.80 = (f32[512]{0:T(512)S(1)}, f32[512]{0:T(512)}, u32[]{:S(2)}) copy-start(f32[512]{0:T(512)} %get-tuple-element.69) | copy-start | bytes 6148
  594.0 31.0 %all-to-all-start.2 = ((bf16[2,1,256,512]{3,0,1,2:T(2,128)(2,1)}), bf16[2,1,256,512]{3,0,1,2:T(2,128)(2,1)S(1)}, u32[]{:S(2)}, u32[]{:S(2)}) async-start(bf16[2,1,256,512]{3,0,1,2:T(2,128)(2,1)} %copy.185), calls=%async_computation.18 | async-start | bytes 1048576 | tf_op jit(solution)/shard_map/all_to_all | solution.py:306
  (70 other events, 231.9 us)
Sparse Core Ops, SparseCore 0:
  58.3 9.0 reduce-scatter.41
  74.0 9.3 reduce-scatter.33
  92.8 16.9 reduce-scatter.35
  112.6 14.3 reduce-scatter.43
  129.1 12.0 reduce-scatter.57
  178.2 17.2 reduce-scatter.45
  197.9 13.2 reduce-scatter.49
  217.1 17.1 reduce-scatter.37
  235.8 14.9 all-gather.14
  252.2 14.8 all-gather.10
  268.6 11.7 all-gather.8
  283.1 15.7 reduce-scatter.59
  301.8 14.5 reduce-scatter.51
  319.0 14.5 reduce-scatter.47
  347.5 8.5 reduce-scatter.53
  358.2 9.6 reduce-scatter.61
  391.4 9.8 all-gather.12
  402.9 10.8 all-gather.16
  415.4 11.7 all-gather.6
  429.9 15.7 reduce-scatter.55
  448.5 14.5 reduce-scatter.63
  466.0 14.5 reduce-scatter.39
  484.1 67.7 reduce-scatter.65
  555.3 77.5 reduce-scatter.73
  637.0 66.7 reduce-scatter.71
  707.8 66.8 reduce-scatter.69
  778.2 148.0 reduce-scatter.67
  930.3 148.0 reduce-scatter.77
  1082.0 147.9 reduce-scatter.75
where the time goes:
time: 1250 us; the launch traced here: 1240 us
  waiting for transfers between devices  693 us (55%)
  matrix products  182 us (15%)
  local copies, waits for them, and re-layouts  140 us (11%)
  blocking collectives  125 us (10%)
  other arithmetic  65.1 us (5%)
  starting transfers between devices  19.2 us (2%)
  between operations  16.4 us (1%)
    unnamed x34, waiting for transfers between devices  443 us
    reduce_scatter x1, waiting for transfers between devices, per_device(): lax.psum_scatter(down_grad_sum.astype(jnp.bfloat16), 'dp', scatter_dimens...  149 us
    unnamed x195, local copies, waits for them, and re-layouts  97.5 us
    all_gather x8, blocking collectives, column_gather(): return lax.all_gather(values, 'col', axis=1, tiled=True)  69 us
    dot_general x2, matrix products, per_device(): jnp.einsum('rd,kre->kde', normed_second_all, pair_grad_all, preferred_ele...  34.9 us
    reduce_scatter x8, waiting for transfers between devices, column_scatter(): lax.psum_scatter(partial_rows.astype(jnp.bfloat16), 'col', scatter_dimens...  34.2 us
    all_gather x6, waiting for transfers between devices, row_gather(): return lax.all_gather(stacked, 'row', axis=2, tiled=True)  31.3 us
    psum x4, blocking collectives, feature_total(): return lax.psum(row_values, ('row', 'col'))  29.1 us
  transfers between devices with their start and end apart: 32, of which 17 were waited for; matrix products, arithmetic and copies ran while one was open for 26% of the time, Pallas kernels for 0%

commit v1 on v0

--- a/solution.py
+++ b/solution.py
@@ -12,6 +12,11 @@
 EPSILON = 1e-05
 ROPE_THETA = 130000.0
 MASKED_SCORE = -1000000000.0
+
+
+def one_after_other(value, axis_one, axis_two):
+    inner = lax.psum(value, axis_one)
+    return lax.psum(inner, axis_two)
 
 
 def rope_tables(slot_count, head_width):
@@ -111,7 +116,7 @@
 
 
 def feature_total(row_values):
-    return lax.psum(row_values, ("row", "col"))
+    return one_after_other(row_values, "row", "col")
 
 
 def norm_scale(values):

time: 1250 us -> 1250 us (level)
    psum x4 -> x8, blocking collectives: 29.1 us -> 32.4 us  [the longest x4 21.1 us: one_after_other(): return lax.psum(inner, axis_two)]
  transfers between devices with their start and end apart: 32 -> 32, of which waited for: 17 -> 18; matrix products, arithmetic and copies ran while one was open for 26% -> 26% of each run, Pallas kernels for 0% -> 0%
where the time goes in v1:
time: 1250 us; the launch traced here: 1240 us
  waiting for transfers between devices  692 us (55%)
  matrix products  182 us (15%)
  local copies, waits for them, and re-layouts  140 us (11%)
  blocking collectives  123 us (10%)
  other arithmetic  65.1 us (5%)
  starting transfers between devices  19 us (2%)
  between operations  16.3 us (1%)
    unnamed x34, waiting for transfers between devices  444 us
    reduce_scatter x1, waiting for transfers between devices, per_device(): lax.psum_scatter(down_grad_sum.astype(jnp.bfloat16), 'dp', scatter_dimens...  149 us
    unnamed x195, local copies, waits for them, and re-layouts  97.8 us
    all_gather x8, blocking collectives, column_gather(): return lax.all_gather(values, 'col', axis=1, tiled=True)  64.5 us
    dot_general x2, matrix products, per_device(): jnp.einsum('rd,kre->kde', normed_second_all, pair_grad_all, preferred_ele...  34.9 us
    reduce_scatter x8, waiting for transfers between devices, column_scatter(): lax.psum_scatter(partial_rows.astype(jnp.bfloat16), 'col', scatter_dimens...  32.5 us
    all_gather x6, waiting for transfers between devices, row_gather(): return lax.all_gather(stacked, 'row', axis=2, tiled=True)  31.2 us
  transfers between devices with their start and end apart: 32, of which 18 were waited for; matrix products, arithmetic and copies ran while one was open for 26% of the time, Pallas kernels for 0%

profile of v1, /device:TPU:0, one launch (start us, length us, event | category | flops | bytes accessed | tf_op | source)
XLA Modules:
  0.0 1238.1 jit_solution(9086319141018543188)
XLA Ops:
  11.4 7.3 all-to-all-start
  41.6 7.9 all_gather.52
  50.3 6.3 convolution_bitcast_fusion.4
  56.7 7.0 all_gather.48
  64.5 6.7 convolution_bitcast_fusion.5
  100.3 10.8 all_gather.60
  111.8 7.8 convolution_bitcast_fusion.2
  119.7 12.0 copy.158
  131.7 12.3 copy.159
  149.0 5.6 all-reduce.4
  157.8 7.9 all_gather.54
  166.5 10.2 convolution_bitcast_fusion
  176.8 7.0 all_gather.56
  184.7 9.7 convolution_bitcast_fusion.3
  195.3 7.0 all_gather.50
  203.1 11.7 convolution_bitcast_fusion.1
  221.9 10.0 reduce-scatter.38.cloned.1.call-done
  232.0 4.9 multiply_convert_fusion.5
  239.2 9.2 all-gather.15.cloned.1.call-done
  248.5 10.1 fusion.24
  258.6 6.1 all-gather.11.cloned.1.call-done
  264.7 10.1 fusion.23
  278.1 7.2 fusion.20
  285.3 11.2 reduce-scatter.60.cloned.1.call-done
  296.5 17.5 %reduce-scatter.52.cloned.1.call-done = bf16[256,512]{1,0:T(8,128)(2,1)} async-done(((bf16[256,1024]{1,0:T(8,128)(2,1)}), bf16[256,512]{1,0:T(8,128)(2,1)}) %reduce-scatter.52.cloned.1.call-update) | async-done | bytes 262160 | tf_op jit(solution)/shard_map/reduce_scatter | solution.py:113
  319.3 5.6 all-reduce.3
  333.8 8.7 all_gather.58
  345.1 8.1 all_gather.62
  401.3 5.3 fusion.15
  411.4 5.3 fusion.16
  416.7 8.0 all-gather.7.cloned.1.call-done
  424.8 7.2 fusion.17
  456.5 9.3 fusion.5
  465.8 11.7 add_convert_fusion.1
  478.6 15.7 %fusion.74 = f32[2,4096,1024]{2,1,0:T(8,128)} fusion(bf16[2,256,4096]{1,2,0:T(8,128)(2,1)} %all-gather.11.cloned.1.call-done, bf16[256,1024]{1,0:T(8,128)(2,1)S(1)} %copy-done.32), kind=kOutput, calls=%fused_computation.147 | convolution fusion | flops 4294967296 | bytes 38273024 | tf_op jit(solution)/shard_map/rd,kre->kde/dot_general | solution.py:230
  494.3 19.1 %fusion = bf16[2,1024,4096]{1,2,0:T(8,128)(2,1)} fusion(f32[2,4096,1024]{2,1,0:T(8,128)} %fusion.74, bf16[2,256,4096]{1,2,0:T(8,128)(2,1)S(1)} %copy-done.23, bf16[256,1024]{1,0:T(8,128)(2,1)S(1)} %copy-done.30), kind=kOutput, calls=%fused_computation.5 | convolution fusion | flops 4311744512 | bytes 55050240 | tf_op jit(solution)/shard_map/rd,kre->kde/dot_general | solution.py:230
  513.5 11.8 slice_bitcast_fusion
  525.2 11.3 copy.220
  536.6 11.8 copy.218
  561.3 5.9 all-to-all-start.1
  569.9 21.5 %all-to-all-done.1 = bf16[2,1,256,512]{3,0,1,2:T(2,128)(2,1)S(1)} async-done(((bf16[2,1,256,512]{3,0,1,2:T(2,128)(2,1)}), bf16[2,1,256,512]{3,0,1,2:T(2,128)(2,1)S(1)}, u32[]{:S(2)}, u32[]{:S(2)}) %all-to-all-start.1) | async-done | bytes 524320 | tf_op jit(solution)/shard_map/all_to_all | solution.py:308
  598.2 22.2 %all-reduce.10 = (bf16[512]{0:T(512)(128)(2,1)S(1)}, bf16[512]{0:T(512)(128)(2,1)S(1)}) all-reduce(bf16[512]{0:T(512)(128)(2,1)S(1)} %add_convert_fusion.15, bf16[512]{0:T(512)(128)(2,1)S(1)} %add_convert_fusion.14), channel_id=18, replica_groups=mesh['dp'=8,'row'=2,'col'=2] {'dp'}, use_global_device_ids=true, to_apply=%region_49.51.clone | all-reduce | flops 1024 | bytes 4096
  624.0 6.5 reduce-scatter.74.cloned.1.call-done
  632.6 68.9 %reduce-scatter.72.cloned.1.call-done = bf16[128,1024]{1,0:T(8,128)(2,1)} async-done(((bf16[1024,1024]{1,0:T(8,128)(2,1)}), bf16[128,1024]{1,0:T(8,128)(2,1)}) %reduce-scatter.72.cloned.1.call-update) | async-done | bytes 262160
  703.6 68.8 %reduce-scatter.70.cloned.1.call-done = bf16[128,1024]{1,0:T(8,128)(2,1)} async-done(((bf16[1024,1024]{1,0:T(8,128)(2,1)}), bf16[128,1024]{1,0:T(8,128)(2,1)}) %reduce-scatter.70.cloned.1.call-update) | async-done | bytes 262160
  774.5 149.4 %reduce-scatter.68.cloned.1.call-done = bf16[512,1024]{1,0:T(8,128)(2,1)} async-done(((bf16[4096,1024]{1,0:T(8,128)(2,1)}), bf16[512,1024]{1,0:T(8,128)(2,1)}) %reduce-scatter.68.cloned.1.call-update) | async-done | bytes 1048592 | tf_op jit(solution)/shard_map/reduce_scatter | solution.py:303
  926.7 149.4 %reduce-scatter.78.cloned.1.call-done = bf16[128,4096]{1,0:T(8,128)(2,1)} async-done(((bf16[1024,4096]{1,0:T(8,128)(2,1)}), bf16[128,4096]{1,0:T(8,128)(2,1)}) %reduce-scatter.78.cloned.1.call-update) | async-done | bytes 1048592
  1079.3 148.5 %reduce-scatter.76.cloned.1.call-done = bf16[128,4096]{1,0:T(8,128)(2,1)} async-done(((bf16[1024,4096]{1,0:T(8,128)(2,1)}), bf16[128,4096]{1,0:T(8,128)(2,1)}) %reduce-scatter.76.cloned.1.call-update) | async-done | bytes 1048592
  (390 shorter events, 218.1 us)
Async XLA Ops:
  7.2 81.8 %copy-start = (bf16[1024,1024]{1,0:T(8,128)(2,1)S(1)}, bf16[1024,1024]{1,0:T(8,128)(2,1)}, u32[]{:S(2)}) copy-start(bf16[1024,1024]{1,0:T(8,128)(2,1)} %param.22) | copy-start | bytes 6291460
  11.4 21.7 %all-to-all-start = ((bf16[2,8,32,512]{3,2,0,1:T(8,128)(2,1)}), bf16[2,8,32,512]{3,2,0,1:T(8,128)(2,1)S(1)}, u32[]{:S(2)}, u32[]{:S(2)}) async-start(bf16[2,8,32,512]{3,2,0,1:T(8,128)(2,1)} %copy.151), calls=%async_computation | async-start | bytes 1048576 | tf_op jit(solution)/shard_map/all_to_all | solution.py:153
  18.6 60.1 %reduce-scatter.42.cloned.1.call-start = ((), (), s32[]{:S(2)}) async-start(), calls=%async_computation.31 | async-start | bytes 4718592 | tf_op jit(solution)/shard_map/reduce_scatter | solution.py:105
  26.6 14.8 %copy-start.63 = (f32[512]{0:T(512)S(1)}, f32[512]{0:T(512)}, u32[]{:S(2)}) copy-start(f32[512]{0:T(512)} %param.18) | copy-start | bytes 6148
  56.7 24.7 %reduce-scatter.34.cloned.1.call-start = ((), (), s32[]{:S(2)}) async-start(), calls=%async_computation.26 | async-start | bytes 4718592 | tf_op jit(solution)/shard_map/reduce_scatter | solution.py:105
  71.3 72.7 %reduce-scatter.36.cloned.1.call-start = ((), (), s32[]{:S(2)}) async-start(), calls=%async_computation.27 | async-start | bytes 786432 | tf_op jit(solution)/shard_map/reduce_scatter | solution.py:113
  76.4 22.6 %copy-start.69 = (f32[256]{0:T(256)}, f32[256]{0:T(256)S(1)}, u32[]{:S(2)}) copy-start(f32[256]{0:T(256)S(1)} %get-tuple-element.160) | copy-start | bytes 3076
  76.5 22.6 %copy-start.71 = (f32[256]{0:T(256)}, f32[256]{0:T(256)S(1)}, u32[]{:S(2)}) copy-start(f32[256]{0:T(256)S(1)} %get-tuple-element.161) | copy-start | bytes 3076
  90.5 53.5 %reduce-scatter.44.cloned.1.call-start = ((), (), s32[]{:S(2)}) async-start(), calls=%async_computation.32 | async-start | bytes 786432 | tf_op jit(solution)/shard_map/reduce_scatter | solution.py:113
  99.0 116.4 %reduce-scatter.58.cloned.1.call-start = ((), (), s32[]{:S(2)}) async-start(), calls=%async_computation.42 | async-start | bytes 6291456 | tf_op jit(solution)/shard_map/reduce_scatter | solution.py:105
  119.7 95.7 %reduce-scatter.46.cloned.1.call-start = ((), (), s32[]{:S(2)}) async-start(), calls=%async_computation.33 | async-start | bytes 12582912 | tf_op jit(solution)/shard_map/reduce_scatter | solution.py:105
  131.7 24.2 %copy-start.59 = (f32[512]{0:T(512)S(1)}, f32[512]{0:T(512)}, u32[]{:S(2)}) copy-start(f32[512]{0:T(512)} %param.23) | copy-start | bytes 6148
  176.8 45.1 %reduce-scatter.50.cloned.1.call-start = ((), (), s32[]{:S(2)}) async-start(), calls=%async_computation.36 | async-start | bytes 6291456 | tf_op jit(solution)/shard_map/reduce_scatter | solution.py:105
  194.4 37.6 %reduce-scatter.38.cloned.1.call-start = ((), (), s32[]{:S(2)}) async-start(), calls=%async_computation.28 | async-start | bytes 12582912 | tf_op jit(solution)/shard_map/reduce_scatter | solution.py:105
  214.9 33.6 %all-gather.15.cloned.1.call-start = ((), (), s32[]{:S(2)}) async-start(), calls=%async_computation.43 | async-start | bytes 6291456 | tf_op jit(solution)/shard_map/all_gather | solution.py:109
  221.9 42.9 %all-gather.11.cloned.1.call-start = ((), (), s32[]{:S(2)}) async-start(), calls=%async_computation.37 | async-start | bytes 6291456 | tf_op jit(solution)/shard_map/all_gather | solution.py:109
  238.4 39.6 %all-gather.9.cloned.1.call-start = ((), (), s32[]{:S(2)}) async-start(), calls=%async_computation.34 | async-start | bytes 3145728 | tf_op jit(solution)/shard_map/all_gather | solution.py:109
  239.2 57.3 %reduce-scatter.60.cloned.1.call-start = ((), (), s32[]{:S(2)}) async-start(), calls=%async_computation.44 | async-start | bytes 786432 | tf_op jit(solution)/shard_map/reduce_scatter | solution.py:113
  258.6 55.4 %reduce-scatter.52.cloned.1.call-start = ((), (), s32[]{:S(2)}) async-start(), calls=%async_computation.38 | async-start | bytes 786432 | tf_op jit(solution)/shard_map/reduce_scatter | solution.py:113
  274.9 39.1 %copy-start.10 = (bf16[256,512]{1,0:T(8,128)(2,1)S(1)}, bf16[256,512]{1,0:T(8,128)(2,1)}, u32[]{:S(2)}) copy-start(bf16[256,512]{1,0:T(8,128)(2,1)} %reduce-scatter.44.cloned.1.call-done) | copy-start | bytes 786436
  274.9 56.3 %reduce-scatter.48.cloned.1.call-start = ((), (), s32[]{:S(2)}) async-start(), calls=%async_computation.35 | async-start | bytes 786432 | tf_op jit(solution)/shard_map/reduce_scatter | solution.py:113
  285.2 72.9 %reduce-scatter.54.cloned.1.call-start = ((), (), s32[]{:S(2)}) async-start(), calls=%async_computation.39 | async-start | bytes 1572864 | tf_op jit(solution)/shard_map/reduce_scatter | solution.py:105
  345.1 22.8 %reduce-scatter.62.cloned.1.call-start = ((), (), s32[]{:S(2)}) async-start(), calls=%async_computation.45 | async-start | bytes 1572864 | tf_op jit(solution)/shard_map/reduce_scatter | solution.py:105
  355.8 45.5 %all-gather.13.cloned.1.call-start = ((), (), s32[]{:S(2)}) async-start(), calls=%async_computation.40 | async-start | bytes 2359296 | tf_op jit(solution)/shard_map/all_gather | solution.py:109
  388.9 22.4 %all-gather.17.cloned.1.call-start = ((), (), s32[]{:S(2)}) async-start(), calls=%async_computation.46 | async-start | bytes 2359296 | tf_op jit(solution)/shard_map/all_gather | solution.py:109
  400.5 24.3 %all-gather.7.cloned.1.call-start = ((), (), s32[]{:S(2)}) async-start(), calls=%async_computation.29 | async-start | bytes 3145728 | tf_op jit(solution)/shard_map/all_gather | solution.py:109
  401.2 147.3 %reduce-scatter.56.cloned.1.call-start = ((), (), s32[]{:S(2)}) async-start(), calls=%async_computation.41 | async-start | bytes 786432 | tf_op jit(solution)/shard_map/reduce_scatter | solution.py:113
  406.6 142.0 %reduce-scatter.64.cloned.1.call-start = ((), (), s32[]{:S(2)}) async-start(), calls=%async_computation.47 | async-start | bytes 786432 | tf_op jit(solution)/shard_map/reduce_scatter | solution.py:113
  416.7 15.6 %copy-start.21 = (bf16[256,1024]{1,0:T(8,128)(2,1)S(1)}, bf16[256,1024]{1,0:T(8,128)(2,1)}, u32[]{:S(2)}) copy-start(bf16[256,1024]{1,0:T(8,128)(2,1)} %copy-done.20) | copy-start | bytes 1572868
  416.7 141.6 %reduce-scatter.40.cloned.1.call-start = ((), (), s32[]{:S(2)}) async-start(), calls=%async_computation.30 | async-start | bytes 786432 | tf_op jit(solution)/shard_map/reduce_scatter | solution.py:113
  432.0 164.4 %reduce-scatter.66.cloned.1.call-start = ((), (), s32[]{:S(2)}) async-start(), calls=%async_computation.48 | async-start | bytes 2359296 | tf_op jit(solution)/shard_map/reduce_scatter | solution.py:291
  435.3 195.2 %reduce-scatter.74.cloned.1.call-start = ((), (), s32[]{:S(2)}) async-start(), calls=%async_computation.52 | async-start | bytes 2359296
  448.3 253.2 %reduce-scatter.72.cloned.1.call-start = ((), (), s32[]{:S(2)}) async-start(), calls=%async_computation.51 | async-start | bytes 2359296
  452.3 320.1 %reduce-scatter.70.cloned.1.call-start = ((), (), s32[]{:S(2)}) async-start(), calls=%async_computation.50 | async-start | bytes 2359296
  455.0 10.9 copy-start.18
  455.0 468.9 %reduce-scatter.68.cloned.1.call-start = ((), (), s32[]{:S(2)}) async-start(), calls=%async_computation.49 | async-start | bytes 9437184 | tf_op jit(solution)/shard_map/reduce_scatter | solution.py:303
  477.6 16.8 %copy-start.30 = (bf16[256,1024]{1,0:T(8,128)(2,1)S(1)}, bf16[256,1024]{1,0:T(8,128)(2,1)}, u32[]{:S(2)}) copy-start(bf16[256,1024]{1,0:T(8,128)(2,1)} %copy-done.29) | copy-start | bytes 1572868
  477.6 598.5 %reduce-scatter.78.cloned.1.call-start = ((), (), s32[]{:S(2)}) async-start(), calls=%async_computation.54 | async-start | bytes 9437184
  478.6 15.7 %copy-start.23 = (bf16[2,256,4096]{1,2,0:T(8,128)(2,1)S(1)}, bf16[2,256,4096]{1,2,0:T(8,128)(2,1)}, u32[]{:S(2)}) copy-start(bf16[2,256,4096]{1,2,0:T(8,128)(2,1)} %all-gather.15.cloned.1.call-done) | copy-start | bytes 12582916
  536.6 691.2 %reduce-scatter.76.cloned.1.call-start = ((), (), s32[]{:S(2)}) async-start(), calls=%async_computation.53 | async-start | bytes 9437184
  548.5 9.8 copy-start.11
  548.5 9.8 copy-start.22
  548.5 11.4 copy-start.39
  561.3 30.1 %all-to-all-start.1 = ((bf16[2,1,256,512]{3,0,1,2:T(2,128)(2,1)}), bf16[2,1,256,512]{3,0,1,2:T(2,128)(2,1)S(1)}, u32[]{:S(2)}, u32[]{:S(2)}) async-start(bf16[2,1,256,512]{3,0,1,2:T(2,128)(2,1)} %copy.161), calls=%async_computation.9 | async-start | bytes 1048576 | tf_op jit(solution)/shard_map/all_to_all | solution.py:308
  568.1 27.0 %copy-start.85 = (u32[32]{0:T(128)S(1)}, u32[32]{0:T(128)}, u32[]{:S(2)}) copy-start(u32[32]{0:T(128)} %constant.126) | copy-start | bytes 388
  568.1 28.3 %copy-start.79 = (f32[512]{0:T(512)S(1)}, f32[512]{0:T(512)}, u32[]{:S(2)}) copy-start(f32[512]{0:T(512)} %get-tuple-element.60) | copy-start | bytes 6148
  568.1 28.3 %copy-start.80 = (f32[512]{0:T(512)S(1)}, f32[512]{0:T(512)}, u32[]{:S(2)}) copy-start(f32[512]{0:T(512)} %get-tuple-element.69) | copy-start | bytes 6148
  591.4 30.8 %all-to-all-start.2 = ((bf16[2,1,256,512]{3,0,1,2:T(2,128)(2,1)}), bf16[2,1,256,512]{3,0,1,2:T(2,128)(2,1)S(1)}, u32[]{:S(2)}, u32[]{:S(2)}) async-start(bf16[2,1,256,512]{3,0,1,2:T(2,128)(2,1)} %copy.185), calls=%async_computation.18 | async-start | bytes 1048576 | tf_op jit(solution)/shard_map/all_to_all | solution.py:311
  (70 other events, 228.1 us)
Sparse Core Ops, SparseCore 0:
  56.8 9.9 reduce-scatter.41
  71.4 9.8 reduce-scatter.33
  90.7 17.1 reduce-scatter.35
  110.6 14.2 reduce-scatter.43
  127.1 12.0 reduce-scatter.57
  176.9 16.6 reduce-scatter.45
  195.9 13.2 reduce-scatter.49
  215.0 16.9 reduce-scatter.37
  233.5 14.8 all-gather.14
  249.8 14.8 all-gather.10
  266.3 11.7 all-gather.8
  280.7 15.7 reduce-scatter.59
  299.4 14.5 reduce-scatter.51
  316.6 14.5 reduce-scatter.47
  345.2 8.5 reduce-scatter.53
  355.9 9.6 reduce-scatter.61
  389.1 9.7 all-gather.12
  400.6 10.7 all-gather.16
  413.0 11.7 all-gather.6
  427.5 15.7 reduce-scatter.55
  446.1 14.5 reduce-scatter.63
  463.6 14.5 reduce-scatter.39
  481.7 67.7 reduce-scatter.65
  552.9 77.5 reduce-scatter.73
  634.6 66.8 reduce-scatter.71
  705.5 66.8 reduce-scatter.69
  775.9 147.9 reduce-scatter.67
  927.9 148.0 reduce-scatter.77
  1079.7 148.0 reduce-scatter.75
